TPU v7x, 256 devices: a whole 4x4x8 slice. The times are simulated.
256 devices in a mesh: occ: 8 (over z_hi, core), aux: 32 (over x, z_lo, y).
Axes of the slice: x: 4, y: 4, z: 8 (z_hi: 4, z_lo: 2; z = z_hi * 2 + z_lo), core: 2. Of those that a mesh axis runs over, the one named last changes fastest.
Arguments:
- coeffs: bfloat16 [8, 256, 131072], P('occ', None, 'aux'), may hold values from -0.31445312 to 0.31445312
- occ_energy: bfloat16 [8], P('occ'), may hold values from -1.5 to -0.29882812
- virt_energy: bfloat16 [256], replicated, may hold values from 0.19921875 to 3
- screen: int32 [8, 1024], P('occ', 'aux'), may hold values 0 or 1
- owner: int32 [1024], P('aux'), may hold values from 0 to 127
- positions: float32 [3, 128], replicated, may hold values from -1 to 1
Outputs:
- gamma: bfloat16 [8, 256, 131072], P('occ', None, 'aux')
- virial: float32 [9, 131072], P(None, 'aux')
All inputs are finite; a program needn't handle non-finite values. No bound on the sum of `screen` on one device may be relied on, other than what follows from the above.
Results may differ from a plain program's by a relative error of at most 0.0049.
Values may be sent and summed in bfloat16 or wider, within the bound.
A program may use at most 64 MiB of HBM per device.

v0:
```python
import jax
import jax.numpy as jnp
from jax import lax
from jax.sharding import PartitionSpec as P

ABLK = 128


def body(coeffs, occ_energy, virt_energy, screen, owner, positions):
    occ_dev, virt, aux_dev = coeffs.shape
    column_mask = jnp.repeat(screen[0], ABLK).astype(jnp.bfloat16)
    masked = coeffs * column_mask[None, None, :]
    whole, energies = (
        lax.all_gather(masked, "occ", axis=0, tiled=True),
        lax.all_gather(occ_energy, "occ", axis=0, tiled=True),
    )
    all_rows = whole.reshape(-1, aux_dev)
    local = masked.reshape(-1, aux_dev)
    virt_f = virt_energy.astype(jnp.float32)
    spread_local = (virt_f[None, :] - occ_energy.astype(jnp.float32)[:, None]).reshape(-1)
    spread_all = (virt_f[None, :] - energies.astype(jnp.float32)[:, None]).reshape(-1)
    contract_last = (((1,), (1,)), ((), ()))
    contract_first = (((0,), (0,)), ((), ()))
    summed = lax.psum(
        lax.dot_general(all_rows, local, contract_last, preferred_element_type=jnp.float32), "aux"
    )
    amps = (summed / (spread_all[:, None] + spread_local[None, :])).astype(jnp.bfloat16)
    gamma = lax.dot_general(amps, all_rows, contract_first, preferred_element_type=jnp.float32)
    gamma_out = gamma.astype(jnp.bfloat16)
    partial_weight = jnp.sum(gamma_out.astype(jnp.float32) * local.astype(jnp.float32), axis=0)
    weight = lax.psum(partial_weight, "occ")
    atom_ids = jnp.arange(positions.shape[1], dtype=jnp.int32)
    onehot = (owner[:, None] == atom_ids[None, :]).astype(jnp.float32)
    block_where = jnp.dot(onehot, positions.T, precision=lax.Precision.HIGHEST)
    where = jnp.repeat(block_where.T, ABLK, axis=1)
    virial = (where[:, None, :] * where[None, :, :]).reshape(9, aux_dev) * weight[None, :]
    return (gamma_out.reshape(occ_dev, virt, aux_dev), virial)


def solution(mesh):
    placed = (P("occ", None, "aux"), P("occ"), P(), P("occ", "aux"), P("aux"), P())
    return jax.shard_map(
        body,
        mesh=mesh,
        in_specs=placed,
        out_specs=(P("occ", None, "aux"), P(None, "aux")),
        check_vma=False,
    )
```

profile of v0, /device:TPU:8, one launch (start us, length us, event | category | flops | bytes accessed | tf_op | source)
XLA Modules:
  0.0 545.0 jit_solution(9232543608155774374)
XLA Ops:
  7.2 0.0 copy-start
  7.2 0.0 all-gather.2.cloned.1.call-start
  7.2 0.7 convert_bitcast_fusion
  7.9 0.1 broadcast_bitcast_fusion.1
  8.0 3.1 broadcast_multiply_fusion
  11.0 0.0 copy-start.1
  11.0 0.0 all-gather.2.cloned.1.call-update
  11.0 0.0 all-reduce.3.cloned.1.call-start
  11.1 160.1 %all-gather.2.cloned.1.call-done = bf16[8,256,4096]{2,1,0:T(8,128)(2,1)} async-done(((bf16[1,256,4096]{2,1,0:T(8,128)(2,1)}), bf16[8,256,4096]{2,1,0:T(8,128)(2,1)}) %all-gather.2.cloned.1.call-update) | async-done | bytes 16777232 | tf_op jit(solution)/shard_map/all_gather | solution.py:14
  171.2 0.0 copy-done.1
  171.2 9.6 %fusion = f32[2048,256]{1,0:T(8,128)} fusion(bf16[2048,4096]{1,0:T(8,128)(2,1)} %bitcast.29, bf16[1,256,4096]{2,1,0:T(8,128)(2,1)S(1)} %copy-done.1), kind=kOutput, calls=%fused_computation.2 | convolution fusion | flops 4294967296 | bytes 20971520 | tf_op jit(solution)/shard_map/dot_general | solution.py:25
  180.8 0.0 copy-start.4
  180.8 0.0 copy-start.2
  180.8 0.0 copy-start.3
  180.8 0.0 all-reduce.3.cloned.1.call-update
  181.5 0.0 copy-done.4
  181.5 0.6 dynamic-slice
  182.1 0.7 dynamic-update-slice
  182.8 16.4 %all-reduce = bf16[8]{0:T(256)(128)(2,1)S(1)} all-reduce(bf16[8]{0:T(256)(128)(2,1)S(1)} %dynamic-update-slice), channel_id=1, replica_groups=mesh['occ'=8,'aux'=32] {'occ'}, use_global_device_ids=true, to_apply=%add | all-reduce | flops 8 | bytes 32
  199.2 0.0 copy-done.2
  199.2 0.1 subtract_bitcast_fusion
  199.3 0.0 copy-done
  199.3 0.0 copy-done.3
  199.3 0.2 convolution_bitcast_fusion
  199.5 0.1 broadcast_bitcast_fusion
  199.6 0.1 copy.11
  199.7 0.1 mul.44
  199.8 297.7 %all-reduce.3.cloned.1.call-done = f32[2048,256]{1,0:T(8,128)} async-done(((f32[2048,256]{1,0:T(8,128)}), f32[2048,256]{1,0:T(8,128)}) %all-reduce.3.cloned.1.call-update) | async-done | bytes 2097168 | tf_op jit(solution)/shard_map/psum | solution.py:24
  497.5 12.8 %multiply_reduce_fusion = (f32[4096]{0:T(1024)S(1)}, bf16[256,4096]{1,0:T(8,128)(2,1)}) fusion(bf16[1,256,4096]{2,1,0:T(8,128)(2,1)S(1)} %copy-done.1, bf16[2048,4096]{1,0:T(8,128)(2,1)} %bitcast.30, f32[2048,256]{1,0:T(8,128)} %all-reduce.3.cloned.1.call-done, f32[256]{0:T(256)S(1)} %broadcast_subtract_fusion, f32[2048]{0:T(1024)S(1)} %bitcast.28), kind=kOutput, calls=%fused_computation.1 | convolution fusion | flops 4301778944 | bytes 23094272 | tf_op jit(solution)/shard_map/dot_general | solution.py:28
  510.3 27.1 %psum.15 = f32[4096]{0:T(1024)S(1)} all-reduce(f32[4096]{0:T(1024)S(1)} %get-tuple-element.2), channel_id=1, replica_groups=mesh['occ'=8,'aux'=32] {'occ'}, use_global_device_ids=true, to_apply=%region_2.0 | all-reduce | flops 4096 | bytes 32768 | tf_op jit(solution)/shard_map/psum | solution.py:31
  537.4 0.7 broadcast_multiply_fusion.1
  (6 shorter events, 0.1 us)
Async XLA Ops:
  7.2 192.1 %copy-start = (f32[3,128]{1,0:T(4,128)S(1)}, f32[3,128]{1,0:T(4,128)}, u32[]{:S(2)}) copy-start(f32[3,128]{1,0:T(4,128)} %param.11) | copy-start | bytes 4612
  7.2 164.0 %all-gather.2.cloned.1.call-start = ((), (), s32[]{:S(2)}) async-start(), calls=%async_computation | async-start | bytes 18874368 | tf_op jit(solution)/shard_map/all_gather | solution.py:14
  11.0 160.2 %copy-start.1 = (bf16[1,256,4096]{2,1,0:T(8,128)(2,1)S(1)}, bf16[1,256,4096]{2,1,0:T(8,128)(2,1)}, u32[]{:S(2)}) copy-start(bf16[1,256,4096]{2,1,0:T(8,128)(2,1)} %broadcast_multiply_fusion) | copy-start | bytes 6291460
  11.0 486.4 %all-reduce.3.cloned.1.call-start = ((), (), s32[]{:S(2)}) async-start(), calls=%async_computation.1 | async-start | bytes 4194304 | tf_op jit(solution)/shard_map/psum | solution.py:24
  180.8 0.7 copy-start.4
  180.8 18.4 %copy-start.2 = (bf16[256]{0:T(256)(128)(2,1)S(1)}, bf16[256]{0:T(256)(128)(2,1)}, u32[]{:S(2)}) copy-start(bf16[256]{0:T(256)(128)(2,1)} %param.8) | copy-start | bytes 1540
  180.8 18.5 %copy-start.3 = (s32[32]{0:T(128)S(1)}, s32[32]{0:T(128)}, u32[]{:S(2)}) copy-start(s32[32]{0:T(128)} %param.10) | copy-start | bytes 388
Sparse Core Ops, SparseCore 0:
  11.2 159.9 all-gather.1
  181.0 316.4 all-reduce.2
where the time goes:
time: 545 us
  waiting for transfers between devices  458 us (84%)
  blocking collectives  43.5 us (8%)
  matrix products  22.6 us (4%)
  between operations  14.8 us (3%)
    psum x1, waiting for transfers between devices, body(): lax.psum(lax.dot_general(all_rows, local, contract_last, preferred_elemen...  298 us
    all_gather x1, waiting for transfers between devices, body(): lax.all_gather(masked, 'occ', axis=0, tiled=True)  160 us
    psum x1, blocking collectives, body(): weight = lax.psum(partial_weight, 'occ')  27.1 us
    unnamed x1, blocking collectives  16.4 us
    dot_general x1, matrix products, body(): lax.dot_general(amps, all_rows, contract_first, preferred_element_type=jn...  12.8 us
  transfers between devices with their start and end apart: 2, of which 2 were waited for; matrix products, arithmetic and copies ran while one was open for 0% of the time, Pallas kernels for 0%

commit v1 on v0

--- a/solution.py
+++ b/solution.py
@@ -11,7 +11,9 @@
     column_mask = jnp.repeat(screen[0], ABLK).astype(jnp.bfloat16)
     masked = coeffs * column_mask[None, None, :]
     whole, energies = (
-        lax.all_gather(masked, "occ", axis=0, tiled=True),
+        jnp.concatenate(
+            lax.all_to_all(jnp.stack([masked] * lax.axis_size("occ")), "occ", 0, 0), axis=0
+        ),
         lax.all_gather(occ_energy, "occ", axis=0, tiled=True),
     )
     all_rows = whole.reshape(-1, aux_dev)

time: 545 us -> 764 us (1.40)
  blocking collectives: 43.5 us -> 417 us
  waiting for transfers between devices: 458 us -> 299 us
  local copies, waits for them, and re-layouts: 1.64 us -> 9.36 us
    all_to_all x0 -> x1, blocking collectives: none -> 376 us  [body(): lax.all_to_all(jnp.stack([masked] * lax.axis_size('occ')), 'occ', 0, 0)]
    all_gather x1 -> x0, waiting for transfers between devices: 160 us -> none  [body(): lax.all_gather(masked, 'occ', axis=0, tiled=True)]
  transfers between devices with their start and end apart: 2 -> 1, of which waited for: 2 -> 1; matrix products, arithmetic and copies ran while one was open for 0% -> 0% of each run, Pallas kernels for 0% -> 0%
where the time goes in v1:
time: 764 us; the launch traced here: 763 us
  blocking collectives  417 us (55%)
  waiting for transfers between devices  299 us (39%)
  matrix products  19.4 us (3%)
  between operations  14.8 us (2%)
  local copies, waits for them, and re-layouts  9.36 us (1%)
    all_to_all x1, blocking collectives, body(): lax.all_to_all(jnp.stack([masked] * lax.axis_size('occ')), 'occ', 0, 0)  376 us
    psum x1, waiting for transfers between devices, body(): lax.psum(lax.dot_general(all_rows, local, contract_last, preferred_elemen...  299 us
    psum x1, blocking collectives, body(): weight = lax.psum(partial_weight, 'occ')  27.1 us
  transfers between devices with their start and end apart: 1, of which 1 were waited for; matrix products, arithmetic and copies ran while one was open for 0% of the time, Pallas kernels for 0%

profile of v1, /device:TPU:8, one launch (start us, length us, event | category | flops | bytes accessed | tf_op | source)
XLA Modules:
  0.0 763.3 jit_solution(15056371594196600784)
XLA Ops:
  7.2 0.0 copy-start
  7.2 0.0 all-reduce.3.cloned.1.call-start
  7.2 0.7 convert_bitcast_fusion
  7.9 0.1 broadcast_bitcast_fusion.1
  8.0 1.7 multiply_bitcast_fusion
  9.7 2.0 stack.2
  11.7 375.7 %all_to_all.5 = bf16[8,1,256,4096]{3,2,1,0:T(8,128)(2,1)S(1)} all-to-all(bf16[8,1,256,4096]{3,2,1,0:T(8,128)(2,1)S(1)} %stack.2), channel_id=1, replica_groups=mesh['occ'=8,'aux'=32] {'occ'}, dimensions={0} | all-to-all | bytes 33554432 | tf_op jit(solution)/shard_map/all_to_all | solution.py:15
  387.4 0.0 copy-start.1
  387.4 5.7 copy-done.1
  393.1 6.4 fusion.3
  399.5 0.0 copy-start.4
  399.5 0.0 copy-start.2
  399.5 0.0 copy-start.3
  399.5 0.0 all-reduce.3.cloned.1.call-update
  400.2 0.0 copy-done.4
  400.2 0.6 dynamic-slice
  400.9 0.7 dynamic-update-slice
  401.6 14.2 %all-reduce = bf16[8]{0:T(256)(128)(2,1)S(1)} all-reduce(bf16[8]{0:T(256)(128)(2,1)S(1)} %dynamic-update-slice), channel_id=1, replica_groups=mesh['occ'=8,'aux'=32] {'occ'}, use_global_device_ids=true, to_apply=%add | all-reduce | flops 8 | bytes 32
  415.8 0.0 copy-done.2
  415.8 0.1 subtract_bitcast_fusion
  415.9 0.0 copy-done
  415.9 0.0 copy-done.3
  415.9 0.2 convolution_bitcast_fusion
  416.1 0.1 broadcast_bitcast_fusion
  416.2 0.1 copy.11
  416.3 0.1 mul.47
  416.4 299.4 %all-reduce.3.cloned.1.call-done = f32[2048,256]{1,0:T(8,128)} async-done(((f32[2048,256]{1,0:T(8,128)}), f32[2048,256]{1,0:T(8,128)}) %all-reduce.3.cloned.1.call-update) | async-done | bytes 2097168 | tf_op jit(solution)/shard_map/psum | solution.py:26
  715.8 12.8 %multiply_reduce_fusion = (f32[4096]{0:T(1024)S(1)}, bf16[256,4096]{1,0:T(8,128)(2,1)}) fusion(bf16[256,4096]{1,0:T(8,128)(2,1)S(1)} %multiply_bitcast_fusion, bf16[2048,4096]{1,0:T(8,128)(2,1)} %bitcast.27, f32[2048,256]{1,0:T(8,128)} %all-reduce.3.cloned.1.call-done, f32[256]{0:T(256)S(1)} %broadcast_subtract_fusion, f32[2048]{0:T(1024)S(1)} %bitcast.29), kind=kOutput, calls=%fused_computation.1 | convolution fusion | flops 4301778944 | bytes 23094272 | tf_op jit(solution)/shard_map/dot_general | solution.py:30
  728.6 27.1 %psum.15 = f32[4096]{0:T(1024)S(1)} all-reduce(f32[4096]{0:T(1024)S(1)} %get-tuple-element.2), channel_id=1, replica_groups=mesh['occ'=8,'aux'=32] {'occ'}, use_global_device_ids=true, to_apply=%region_2.0 | all-reduce | flops 4096 | bytes 32768 | tf_op jit(solution)/shard_map/psum | solution.py:33
  755.7 0.7 broadcast_multiply_fusion
  (6 shorter events, 0.1 us)
Async XLA Ops:
  7.2 408.7 %copy-start = (f32[3,128]{1,0:T(4,128)S(1)}, f32[3,128]{1,0:T(4,128)}, u32[]{:S(2)}) copy-start(f32[3,128]{1,0:T(4,128)} %param.11) | copy-start | bytes 4612
  7.2 708.6 %all-reduce.3.cloned.1.call-start = ((), (), s32[]{:S(2)}) async-start(), calls=%async_computation.1 | async-start | bytes 4194304 | tf_op jit(solution)/shard_map/psum | solution.py:26
  387.4 5.7 copy-start.1
  399.5 0.7 copy-start.4
  399.5 16.3 %copy-start.2 = (bf16[256]{0:T(256)(128)(2,1)S(1)}, bf16[256]{0:T(256)(128)(2,1)}, u32[]{:S(2)}) copy-start(bf16[256]{0:T(256)(128)(2,1)} %param.8) | copy-start | bytes 1540
  399.5 16.4 %copy-start.3 = (s32[32]{0:T(128)S(1)}, s32[32]{0:T(128)}, u32[]{:S(2)}) copy-start(s32[32]{0:T(128)} %param.10) | copy-start | bytes 388
Sparse Core Ops, SparseCore 0:
  399.7 316.0 all-reduce.2
